TPU v7x, 768 devices: a whole 4x8x12 slice. The times are simulated.
768 devices in a mesh: tower: 8 (over y_hi, x), shard: 96 (over z, y_lo, core).
Axes of the slice: x: 4, y: 8 (y_hi: 2, y_lo: 4; y = y_hi * 4 + y_lo), z: 12, core: 2. Of those that a mesh axis runs over, the one named last changes fastest.
Arguments:
- out_grad: bfloat16 [24576, 2048], P(('tower', 'shard')), may hold values from -6 to 6
- pooled: bfloat16 [8, 24576, 2048], P('tower', 'shard'), may hold values from -6 to 6
- down_proj: bfloat16 [8, 2048, 256], P('tower'), may hold values from -0.125 to 0.125
- up_proj: bfloat16 [8, 256, 2048], P('tower'), may hold values from -0.375 to 0.375
- cross_bias: float32 [8, 2048], P('tower'), may hold values from -3 to 3
- out_proj: bfloat16 [8, 2048, 256], P('tower'), may hold values from -0.125 to 0.125
- assign: int32 [128], replicated, may hold values from 0 to 127, each once
Outputs:
- feature_grad: bfloat16 [24576, 16384], P(('tower', 'shard'))
- weight_grad: float32 [8, 768, 2048], P('tower', 'shard')
- bias_grad: float32 [8, 2048], P('tower')
Inputs may be any that keep to these rules, and one draw needn't show every extreme that they name: `assign`: slot k of the 128 slots belongs to tower k // 16; every feature sits in exactly one slot.
All inputs are finite; a program needn't handle non-finite values.
Results may differ from a plain program's by a relative error of at most 0.01.
Values may be sent and summed in bfloat16 or wider, within the bound.
A program may use at most 32 MiB of HBM per device.

v0:
```python
import math

import jax
import jax.numpy as jnp
from jax import lax
from jax.sharding import PartitionSpec as P

EMB = 128


def body(out_grad, pooled, down_proj, up_proj, cross_bias, out_proj, assign):
    grad_out = lax.all_to_all(out_grad, "tower", split_axis=1, concat_axis=0, tiled=True)
    feature_in = pooled[0]
    w_down = down_proj[0]
    w_up = up_proj[0]
    w_out = out_proj[0]
    bias_row = cross_bias[0]
    hidden_low = jnp.dot(feature_in, w_down, preferred_element_type=jnp.float32).astype(
        jnp.bfloat16
    )
    gate_full = jnp.dot(hidden_low, w_up, preferred_element_type=jnp.float32) + bias_row[None, :]
    factor = gate_full + 1.0
    crossed = (feature_in * factor).astype(jnp.bfloat16)
    grad_crossed = jnp.einsum(
        "no,wo->nw", grad_out, w_out, preferred_element_type=jnp.float32
    ).astype(jnp.bfloat16)
    grad_gate = grad_crossed.astype(jnp.float32) * feature_in
    grad_gate_low = grad_gate.astype(jnp.bfloat16)
    grad_hidden = jnp.einsum(
        "nw,rw->nr", grad_gate_low, w_up, preferred_element_type=jnp.float32
    ).astype(jnp.bfloat16)
    grad_inputs = (
        grad_crossed.astype(jnp.float32) * factor
        + jnp.einsum("nr,wr->nw", grad_hidden, w_down, preferred_element_type=jnp.float32)
    ).astype(jnp.bfloat16)
    returned = lax.all_to_all(grad_inputs, "tower", split_axis=0, concat_axis=1, tiled=True)
    local_rows = returned.shape[0]
    blocks = returned.reshape(local_rows, -1, EMB)
    inverse = jnp.argsort(assign)
    feature_grad = jnp.take(blocks, inverse, axis=1).reshape(local_rows, -1)
    shards = lax.axis_size("shard")
    weight_scale = 1.0 / math.sqrt(grad_out.shape[0] * shards)
    stacked = jnp.concatenate(
        [
            jnp.einsum("nr,nw->rw", grad_hidden, feature_in, preferred_element_type=jnp.float32),
            jnp.einsum("nr,nw->rw", hidden_low, grad_gate_low, preferred_element_type=jnp.float32),
            jnp.einsum("nr,nw->rw", grad_out, crossed, preferred_element_type=jnp.float32),
        ],
        axis=0,
    )
    summed = lax.psum_scatter(stacked, "shard", scatter_dimension=0, tiled=True)
    weight_grad = (summed * weight_scale)[None]
    bias_grad = lax.psum(jnp.sum(grad_gate, axis=0), "shard")[None]
    return (feature_grad, weight_grad, bias_grad)


def solution(mesh):
    placed = (
        P(("tower", "shard"), None),
        P("tower", "shard", None),
        P("tower", None, None),
        P("tower", None, None),
        P("tower", None),
        P("tower", None, None),
        P(),
    )
    return jax.shard_map(
        body,
        mesh=mesh,
        in_specs=placed,
        out_specs=(P(("tower", "shard"), None), P("tower", "shard", None), P("tower", None)),
        check_vma=False,
    )
```

profile of v0, /device:TPU:1, one launch (start us, length us, event | category | flops | bytes accessed | tf_op | source)
XLA Modules:
  0.0 473.7 jit_solution(12163160734479378378)
XLA Ops:
  7.2 0.0 copy-start
  7.2 0.0 copy-start.6
  7.2 1.7 copy.24
  8.8 10.1 %all-to-all-start = ((bf16[32,8,256]{2,0,1:T(8,128)(2,1)}), bf16[32,8,256]{2,0,1:T(8,128)(2,1)S(1)}, u32[]{:S(2)}, u32[]{:S(2)}) async-start(bf16[32,8,256]{2,0,1:T(8,128)(2,1)} %bitcast.56), calls=%async_computation | async-start | bytes 262144 | tf_op jit(solution)/shard_map/all_to_all | solution.py:12
  18.9 0.0 reduce-scatter.2.cloned.1.call-start
  19.0 2.0 convolution_convert_fusion.2
  21.0 0.0 copy-start.1
  21.0 0.0 copy-start.5
  21.0 0.0 copy-done
  21.0 0.0 copy-done.6
  21.0 1.8 fusion
  22.8 5.6 %all-to-all-done = bf16[32,8,256]{2,0,1:T(8,128)(2,1)S(1)} async-done(((bf16[32,8,256]{2,0,1:T(8,128)(2,1)}), bf16[32,8,256]{2,0,1:T(8,128)(2,1)S(1)}, u32[]{:S(2)}, u32[]{:S(2)}) %all-to-all-start) | async-done | bytes 131104 | tf_op jit(solution)/shard_map/all_to_all | solution.py:12
  28.4 0.0 copy-done.1
  28.4 0.0 copy-done.5
  28.4 0.5 fusion.3
  28.9 0.0 copy-start.4
  28.9 0.5 convolution_convert_fusion.1
  29.4 0.0 copy-start.2
  29.4 0.5 fusion.15
  29.9 0.0 copy-done.4
  29.9 1.1 copy-done.2
  31.0 0.5 convolution_bitcast_fusion
  31.5 0.5 fusion.11
  32.0 3.1 pad_maximum_fusion
  35.1 0.0 copy-start.3
  35.1 0.0 reduce-scatter.2.cloned.1.call-update
  35.1 1.6 copy-done.3
  36.6 3.0 fusion.1
  39.6 0.0 copy-start.7
  39.6 3.7 all-to-all-start.1
  43.3 0.0 copy-done.7
  43.3 2.5 sort.17
  45.9 0.1 broadcast_bitcast_fusion
  46.0 226.7 %psum.7 = f32[1,2048]{1,0:T(1,128)} all-reduce(f32[1,2048]{1,0:T(1,128)S(1)} %bitcast.62), channel_id=1, replica_groups=mesh['tower'=8,'shard'=96] {'shard'}, use_global_device_ids=true, to_apply=%region_3.4 | all-reduce | flops 2048 | bytes 16384 | tf_op jit(solution)/shard_map/psum | solution.py:53
  272.7 0.0 all-to-all-done.1
  272.7 0.6 copy.17
  273.2 0.5 reshape.24
  273.8 0.7 copy.18
  274.5 0.8 gather_fusion
  275.2 1.2 bitcast_select_fusion
  276.4 189.0 %reduce-scatter.2.cloned.1.call-done = f32[8,2048]{1,0:T(8,128)} async-done(((f32[768,2048]{1,0:T(8,128)}), f32[8,2048]{1,0:T(8,128)}) %reduce-scatter.2.cloned.1.call-update) | async-done | bytes 65552 | tf_op jit(solution)/shard_map/reduce_scatter | solution.py:51
  465.4 1.5 multiply_bitcast_fusion
  (4 shorter events, 0.0 us)
Async XLA Ops:
  7.2 13.8 %copy-start = (bf16[1,256,2048]{2,1,0:T(8,128)(2,1)S(1)}, bf16[1,256,2048]{2,1,0:T(8,128)(2,1)}, u32[]{:S(2)}) copy-start(bf16[1,256,2048]{2,1,0:T(8,128)(2,1)} %param.10) | copy-start | bytes 3145732
  7.2 13.8 %copy-start.6 = (f32[1,2048]{1,0:T(1,128)S(1)}, f32[1,2048]{1,0:T(1,128)}, u32[]{:S(2)}) copy-start(f32[1,2048]{1,0:T(1,128)} %param.11) | copy-start | bytes 24580
  8.8 19.5 %all-to-all-start = ((bf16[32,8,256]{2,0,1:T(8,128)(2,1)}), bf16[32,8,256]{2,0,1:T(8,128)(2,1)S(1)}, u32[]{:S(2)}, u32[]{:S(2)}) async-start(bf16[32,8,256]{2,0,1:T(8,128)(2,1)} %bitcast.56), calls=%async_computation | async-start | bytes 262144 | tf_op jit(solution)/shard_map/all_to_all | solution.py:12
  18.9 446.5 %reduce-scatter.2.cloned.1.call-start = ((), (), s32[]{:S(2)}) async-start(), calls=%async_computation.3 | async-start | bytes 6356992 | tf_op jit(solution)/shard_map/reduce_scatter | solution.py:51
  21.0 7.4 %copy-start.1 = (bf16[1,256,2048]{2,1,0:T(8,128)(2,1)S(1)}, bf16[1,256,2048]{2,1,0:T(8,128)(2,1)}, u32[]{:S(2)}) copy-start(bf16[1,256,2048]{2,1,0:T(8,128)(2,1)} %param.8) | copy-start | bytes 3145732
  21.0 7.4 %copy-start.5 = (bf16[1,2048,256]{2,1,0:T(8,128)(2,1)S(1)}, bf16[1,2048,256]{2,1,0:T(8,128)(2,1)}, u32[]{:S(2)}) copy-start(bf16[1,2048,256]{2,1,0:T(8,128)(2,1)} %param.12) | copy-start | bytes 3145732
  28.9 1.0 copy-start.4
  29.4 1.6 copy-start.2
  35.1 1.6 copy-start.3
  39.6 3.7 copy-start.7
  39.6 233.0 %all-to-all-start.1 = ((bf16[8,32,2048]{2,1,0:T(8,128)(2,1)}), bf16[8,32,2048]{2,1,0:T(8,128)(2,1)S(1)}, u32[]{:S(2)}, u32[]{:S(2)}) async-start(bf16[8,32,2048]{2,1,0:T(8,128)(2,1)} %bitcast.58), calls=%async_computation.1 | async-start | bytes 2097152 | tf_op jit(solution)/shard_map/all_to_all | solution.py:36
Sparse Core Ops, SparseCore 0:
  35.2 430.1 reduce-scatter.1
where the time goes:
time: 479 us; the launch traced here: 474 us
  blocking collectives  227 us (47%)
  waiting for transfers between devices  195 us (41%)
  between operations  14.2 us (3%)
  starting transfers between devices  13.8 us (3%)
  matrix products  9.21 us (2%)
  other arithmetic  8.3 us (2%)
  local copies, waits for them, and re-layouts  6.95 us (1%)
    psum x1, blocking collectives, body(): bias_grad = lax.psum(jnp.sum(grad_gate, axis=0), 'shard')[None]  227 us
    reduce_scatter x1, waiting for transfers between devices, body(): summed = lax.psum_scatter(stacked, 'shard', scatter_dimension=0, tiled=True)  189 us
    all_to_all x1, starting transfers between devices, body(): lax.all_to_all(out_grad, 'tower', split_axis=1, concat_axis=0, tiled=True)  10.1 us
  transfers between devices with their start and end apart: 3, of which 2 were waited for; matrix products, arithmetic and copies ran while one was open for 3% of the time, Pallas kernels for 0%

commit v1 on v0

v1 whole, which is shorter than its diff:
```python
import functools
import math

import jax
import jax.numpy as jnp
from jax import lax
from jax.experimental import pallas as pl
from jax.experimental.pallas import tpu as pltpu
from jax.sharding import PartitionSpec as P

MESH = pl.DeviceIdType.MESH
F32 = jnp.float32
BF16 = jnp.bfloat16
NX, NYH, NZ, NYL, NC = 4, 2, 12, 4, 2
TOWERS = NX * NYH
EMB = 128
TILE = 512
LONG, SHORT = 6, 5
NEED = (6, -5, 5, -4, 4, -3, 3, -2, 2, -1, 1, 0)


def dot_nn(a, b):
    return jnp.dot(a, b, preferred_element_type=F32)


def dot_nt(a, b):
    return lax.dot_general(a, b, (((1,), (1,)), ((), ())), preferred_element_type=F32)


def remote(src, dst, send, recv, device):
    return pltpu.make_async_remote_copy(
        src_ref=src, dst_ref=dst, send_sem=send, recv_sem=recv, device_id=device, device_id_type=MESH
    )


def main_kernel(
    scale,
    og_h, x_h, wd_h, wu_h, wo_h, cb_h,
    out_f, out_w, out_b,
    x, wd, wu, wo, cb, go, fac, cr, gc, ggl, gi, part, pair, long_s, long_r, short_s, short_r,
    mine, y_s, y_r, bias, b_pair, b_y, b_z, b_half, b_other,
    in_sem, a1_s, a1_r, a2_s, a2_r, p_s, p_r, l_s, l_r, s_s, s_r, ys_s, ys_r,
    bp_s, bp_r, by_s, by_r, bz_s, bz_r, bf_s, bf_r,
):
    t = lax.axis_index("tower")
    s = lax.axis_index("shard")
    yh, xx = t // NX, t % NX
    z, yl, c = s // (NYL * NC), (s // NC) % NYL, s % NC
    sign = 1 - 2 * c
    rows, width = x.shape
    tiles = width // TILE
    half = width // 2

    def tower_at(i):
        return ((yh + i // NX) % NYH) * NX + (xx + i % NX) % NX

    def shard_at(zz, yy, cc):
        return {"shard": (zz * NYL + yy) * NC + cc}

    order = [i for i in range(NX, TOWERS)] + [i for i in range(1, NX)]
    partner = shard_at(z, yl, 1 - c)
    peers = [{"tower": tower_at(i)} for i in order]
    peers.append(partner)
    peers += [shard_at(z, (yl + j) % NYL, c) for j in range(1, NYL)]
    peers += [shard_at((z + j) % NZ, yl, c) for j in range(1, NZ)]

    barrier = pltpu.get_barrier_semaphore()
    for peer in peers:
        pl.semaphore_signal(barrier, inc=1, device_id=peer, device_id_type=MESH)

    loads = [
        pltpu.make_async_copy(src, dst, in_sem.at[k])
        for k, (src, dst) in enumerate(((x_h, x), (wd_h, wd), (wu_h, wu), (cb_h, cb), (wo_h, wo)))
    ]
    own = pltpu.make_async_copy(
        og_h.at[:, pl.ds(pl.multiple_of(t * 256, 256), 256)], go.at[t], in_sem.at[5]
    )
    for load in loads:
        load.start()
    own.start()
    pl.semaphore_wait(barrier, len(peers))

    first = []
    for i in order:
        dest = tower_at(i)
        first.append(
            remote(
                og_h.at[:, pl.ds(pl.multiple_of(dest * 256, 256), 256)],
                go.at[t], a1_s.at[i], a1_r.at[i], {"tower": dest},
            )
        )
        first[-1].start()

    loads[0].wait()
    loads[1].wait()
    hidden_wide = dot_nn(x[...], wd[...]).astype(BF16)
    hidden_t = hidden_wide.astype(F32).T.astype(BF16)
    loads[2].wait()
    loads[3].wait()

    def forward(k, carry):
        at = pl.ds(pl.multiple_of(k * TILE, TILE), TILE)
        factor = dot_nn(hidden_wide, wu[:, at]) + cb[:, at] + 1.0
        fac[:, at] = factor
        cr[:, at] = (x[:, at].astype(F32) * factor).astype(BF16)
        return carry

    lax.fori_loop(0, tiles, forward, 0)
    loads[4].wait()
    own.wait()
    for copy in first:
        copy.wait_recv()
    grad_out = go[...].reshape(rows, 256)
    grad_out_t = grad_out.astype(F32).T.astype(BF16)

    def crossed_grad(k, total):
        at = pl.ds(pl.multiple_of(k * TILE, TILE), TILE)
        low = dot_nt(grad_out, wo[at, :]).astype(BF16)
        gc[:, at] = low
        gate = low.astype(F32) * x[:, at].astype(F32)
        column = jnp.sum(gate, axis=0, keepdims=True)
        bias[k // (tiles // 2), :, pl.ds(pl.multiple_of((k % (tiles // 2)) * TILE, TILE), TILE)] = column
        gate_low = gate.astype(BF16)
        ggl[:, at] = gate_low
        return total + dot_nt(gate_low, wu[:, at])

    hidden_grad_wide = lax.fori_loop(0, tiles, crossed_grad, jnp.zeros((rows, 256), F32))
    hidden_grad = hidden_grad_wide.astype(BF16)
    hidden_grad_t = hidden_grad.astype(F32).T.astype(BF16)

    def inputs_grad(k, carry):
        at = pl.ds(pl.multiple_of(k * TILE, TILE), TILE)
        value = gc[:, at].astype(F32) * fac[:, at] + dot_nt(hidden_grad, wd[at, :])
        low = value.astype(BF16)
        for a in range(TOWERS):
            for j in range(TILE // EMB):
                gi[a, k * (TILE // EMB) + j] = low[a * 32 : (a + 1) * 32, j * EMB : (j + 1) * EMB]
        return carry

    lax.fori_loop(0, tiles, inputs_grad, 0)
    second = []
    for i in order:
        dest = tower_at(i)
        second.append(remote(gi.at[dest], out_f.at[t], a2_s.at[i], a2_r.at[i], {"tower": dest}))
        second[-1].start()
    keep = pltpu.make_async_copy(gi.at[t], out_f.at[t], in_sem.at[6])
    keep.start()

    bias_pair = remote(bias.at[1 - c], b_pair, bp_s, bp_r, partner)
    bias_pair.start()

    for p, (left, right) in enumerate(((hidden_grad_t, x), (hidden_t, ggl), (grad_out_t, cr))):

        def weights(k, carry):
            at = pl.ds(pl.multiple_of(k * TILE, TILE), TILE)
            value = dot_nn(left, right[:, at])
            for zz in range(4):
                for h in range(2):
                    for cc in range(NC):
                        base = zz * 64 + h * 32 + cc * 8
                        both = jnp.concatenate([value[base : base + 8], value[base + 16 : base + 24]], axis=0)
                        part[cc, p * 4 + zz, h, :, at] = both.astype(BF16)
            return carry

        lax.fori_loop(0, tiles, weights, 0)

    def chunk(offset, direction):
        return (z + direction * offset + NZ) % NZ

    pieces = []
    for k, offset in enumerate(NEED):
        pieces.append(
            remote(part.at[1 - c, chunk(offset, -sign)], pair.at[k], p_s.at[k], p_r.at[k], partner)
        )
        pieces[-1].start()

    ahead = shard_at((z + sign + NZ) % NZ, yl, c)
    behind = shard_at((z - sign + NZ) % NZ, yl, c)
    ring = []

    def local_sum(k, h):
        return part[c, chunk(NEED[k], sign), h].astype(F32) + pair[k, h].astype(F32)

    arms = {
        "long": (long_s, long_r, l_s, l_r, ahead, LONG),
        "short": (short_s, short_r, s_s, s_r, behind, SHORT),
    }
    sent = {}
    bias_y, bias_z = [], []
    for step in range(LONG):
        for name in ("long", "short"):
            if step < arms[name][5]:
                pieces[NEED.index(LONG - step if name == "long" else step - SHORT)].wait_recv()
        for h in range(2):
            for name, (send_ref, recv_ref, send_sem, recv_sem, device, hops) in arms.items():
                if step >= hops:
                    continue
                k = NEED.index(hops - step if name == "long" else step - hops)
                value = local_sum(k, h)
                if step > 0:
                    sent[name, step - 1, h].wait_recv()
                    value = value + recv_ref[step - 1, h].astype(F32)
                send_ref[step, h] = value.astype(BF16)
                copy = remote(
                    send_ref.at[step, h], recv_ref.at[step, h],
                    send_sem.at[step, h], recv_sem.at[step, h], device,
                )
                copy.start()
                sent[name, step, h] = copy
        if step == 0:
            bias_pair.wait_recv()
            b_y[yl] = bias[c] + b_pair[...]
            for j in range(1, NYL):
                copy = remote(b_y.at[yl], b_y.at[yl], by_s.at[j], by_r.at[j], shard_at(z, (yl + j) % NYL, c))
                copy.start()
                bias_y.append(copy)
        if step == 2:
            for copy in bias_y:
                copy.wait_recv()
            b_z[z] = (b_y[0] + b_y[1]) + (b_y[2] + b_y[3])
            for j in range(1, NZ):
                copy = remote(b_z.at[z], b_z.at[z], bz_s.at[j], bz_r.at[j], shard_at((z + j) % NZ, yl, c))
                copy.start()
                bias_z.append(copy)

    pieces[len(NEED) - 1].wait_recv()
    for h in range(2):
        value = local_sum(len(NEED) - 1, h)
        sent["short", SHORT - 1, h].wait_recv()
        value = value + short_r[SHORT - 1, h].astype(F32)
        sent["long", LONG - 1, h].wait_recv()
        value = value + long_r[LONG - 1, h].astype(F32)
        for yy in range(2):
            eight = value[yy * 8 : (yy + 1) * 8]
            mine[h * 2 + yy] = eight
            y_s[h * 2 + yy] = jnp.concatenate([eight[:, :half], eight[:, half:]], axis=0).astype(BF16)
    last = []
    for j in range(1, NYL):
        to = (yl + j) % NYL
        copy = remote(y_s.at[to], y_r.at[j - 1], ys_s.at[j], ys_r.at[j], shard_at(z, to, c))
        copy.start()
        last.append(copy)

    for copy in bias_z:
        copy.wait_recv()
    total = b_z[0]
    for k in range(1, NZ):
        total = total + b_z[k]
    b_half[...] = total
    bias_final = remote(b_half, b_other, bf_s, bf_r, partner)
    bias_final.start()
    out_b[:, pl.ds(pl.multiple_of(c * half, half), half)] = total

    value = mine[yl]
    for copy in last:
        copy.wait_recv()
    for j in range(NYL - 1):
        got = y_r[j].astype(F32)
        value = value + jnp.concatenate([got[:8], got[8:]], axis=1)
    out_w[...] = value * scale

    bias_final.wait_recv()
    out_b[:, pl.ds(pl.multiple_of((1 - c) * half, half), half)] = b_other[...]

    keep.wait()
    for copy in second:
        copy.wait_recv()
    for copy in first + second + pieces + list(sent.values()) + bias_y + bias_z + last + [bias_pair, bias_final]:
        copy.wait_send()


def place_kernel(assign_ref, f_ref, w_ref, b_ref, out_f, out_w, out_b):
    for k in range(f_ref.shape[0]):
        out_f[:, pl.ds(pl.multiple_of(assign_ref[k] * EMB, EMB), EMB)] = f_ref[k]
    out_w[...] = w_ref[...]
    out_b[...] = b_ref[...]


def body(out_grad, pooled, down_proj, up_proj, cross_bias, out_proj, assign):
    rows, width = pooled.shape[1:]
    any_space = pl.BlockSpec(memory_space=pl.ANY)
    vmem = pl.BlockSpec(memory_space=pltpu.VMEM)
    scale = 1.0 / math.sqrt(rows * lax.axis_size("shard"))
    dma = pltpu.SemaphoreType.DMA
    quarter = width // 2
    moved, weights, bias = pl.pallas_call(
        functools.partial(main_kernel, scale),
        out_shape=(
            jax.ShapeDtypeStruct((TOWERS, width // EMB, 32, EMB), BF16),
            jax.ShapeDtypeStruct((8, width), F32),
            jax.ShapeDtypeStruct((1, width), F32),
        ),
        in_specs=[any_space] * 6,
        out_specs=(any_space, vmem, vmem),
        scratch_shapes=[
            pltpu.VMEM((rows, width), BF16),
            pltpu.VMEM((width, 256), BF16),
            pltpu.VMEM((256, width), BF16),
            pltpu.VMEM((width, 256), BF16),
            pltpu.VMEM((1, width), F32),
            pltpu.VMEM((TOWERS, 32, 256), BF16),
            pltpu.VMEM((rows, width), F32),
            pltpu.VMEM((rows, width), BF16),
            pltpu.VMEM((rows, width), BF16),
            pltpu.VMEM((rows, width), BF16),
            pltpu.VMEM((TOWERS, width // EMB, 32, EMB), BF16),
            pltpu.VMEM((NC, NZ, 2, 16, width), BF16),
            pltpu.VMEM((NZ, 2, 16, width), BF16),
            pltpu.VMEM((LONG, 2, 16, width), BF16),
            pltpu.VMEM((LONG, 2, 16, width), BF16),
            pltpu.VMEM((SHORT, 2, 16, width), BF16),
            pltpu.VMEM((SHORT, 2, 16, width), BF16),
            pltpu.VMEM((NYL, 8, width), F32),
            pltpu.VMEM((NYL, 16, quarter), BF16),
            pltpu.VMEM((NYL - 1, 16, quarter), BF16),
            pltpu.VMEM((2, 1, quarter), F32),
            pltpu.VMEM((1, quarter), F32),
            pltpu.VMEM((NYL, 1, quarter), F32),
            pltpu.VMEM((NZ, 1, quarter), F32),
            pltpu.VMEM((1, quarter), F32),
            pltpu.VMEM((1, quarter), F32),
            dma((7,)),
            dma((TOWERS,)), dma((TOWERS,)), dma((TOWERS,)), dma((TOWERS,)),
            dma((NZ,)), dma((NZ,)),
            dma((LONG, 2)), dma((LONG, 2)), dma((SHORT, 2)), dma((SHORT, 2)),
            dma((NYL,)), dma((NYL,)),
            dma, dma, dma((NYL,)), dma((NYL,)), dma((NZ,)), dma((NZ,)), dma, dma,
        ],
        compiler_params=pltpu.CompilerParams(
            collective_id=0, has_side_effects=True, vmem_limit_bytes=65000 * 1024
        ),
        name="tower_backward",
    )(out_grad, pooled[0], down_proj[0], up_proj[0], out_proj[0], cross_bias)
    feature_grad, weight_grad, bias_grad = pl.pallas_call(
        place_kernel,
        out_shape=(
            jax.ShapeDtypeStruct((32, TOWERS * width), BF16),
            jax.ShapeDtypeStruct((8, width), F32),
            jax.ShapeDtypeStruct((1, width), F32),
        ),
        in_specs=[pl.BlockSpec(memory_space=pltpu.SMEM), vmem, vmem, vmem],
        out_specs=(vmem, vmem, vmem),
        name="place_columns",
    )(assign, moved.reshape(TOWERS * (width // EMB), 32, EMB), weights, bias)
    return (feature_grad, weight_grad[None], bias_grad)


def solution(mesh):
    placed = (
        P(("tower", "shard"), None),
        P("tower", "shard", None),
        P("tower", None, None),
        P("tower", None, None),
        P("tower", None),
        P("tower", None, None),
        P(),
    )
    return jax.shard_map(
        body,
        mesh=mesh,
        in_specs=placed,
        out_specs=(P(("tower", "shard"), None), P("tower", "shard", None), P("tower", None)),
        check_vma=False,
    )
```

time: 479 us -> 75 us (0.16); the launches traced: 474 us -> 74.6 us
  blocking collectives: 227 us -> 0 us
  waiting for transfers between devices: 195 us -> 0 us
  Pallas kernels: 0 us -> 73.9 us
  starting transfers between devices: 13.8 us -> 0 us
  between operations: 14.2 us -> 0.64 us
  matrix products: 9.21 us -> 0 us
  other arithmetic: 8.3 us -> 0 us
  local copies, waits for them, and re-layouts: 6.95 us -> 0 us
    psum x1 -> x0, blocking collectives: 227 us -> none  [body(): bias_grad = lax.psum(jnp.sum(grad_gate, axis=0), 'shard')[None]]
    reduce_scatter x1 -> x0, waiting for transfers between devices: 189 us -> none  [body(): summed = lax.psum_scatter(stacked, 'shard', scatter_dimension=0, tiled=True)]
    pallas_call x0 -> x2, Pallas kernels: none -> 73.9 us  [the longest x1 71.4 us: body(): pl.pallas_call(functools.partial(main_kernel, scale), out_shape=(jax.Shap...]
    all_to_all x2 -> x0, starting transfers between devices: 13.8 us -> none  [the longest x1 10.1 us: body(): lax.all_to_all(out_grad, 'tower', split_axis=1, concat_axis=0, tiled=True)]
    dot_general x8 -> x0, matrix products: 9.21 us -> none  [the longest x1 2.98 us: body(): jnp.einsum('nr,wr->nw', grad_hidden, w_down, preferred_element_type=jnp.f...]
    all_to_all x2 -> x0, waiting for transfers between devices: 5.58 us -> none  [the longest x1 5.57 us: body(): lax.all_to_all(out_grad, 'tower', split_axis=1, concat_axis=0, tiled=True)]
  transfers between devices with their start and end apart: 3 -> 0, of which waited for: 2 -> 0; matrix products, arithmetic and copies ran while one was open for 3% -> 0% of each run, Pallas kernels for 0% -> 0%
where the time goes in v1:
time: 75 us; the launch traced here: 74.6 us
  Pallas kernels  73.9 us (99%)
    pallas_call x1, Pallas kernels, body(): pl.pallas_call(functools.partial(main_kernel, scale), out_shape=(jax.Shap...  71.4 us
    pallas_call x1, Pallas kernels, body(): pl.pallas_call(place_kernel, out_shape=(jax.ShapeDtypeStruct((32, TOWERS...  2.51 us

profile of v1, /device:TPU:1, one launch (start us, length us, event | category | flops | bytes accessed | tf_op | source)
XLA Modules:
  0.0 74.6 jit_solution(14629501025116991019)
XLA Ops:
  0.6 71.4 %tower_backward.1 = (bf16[8,16,32,128]{3,2,1,0:T(8,128)(2,1)}, f32[8,2048]{1,0:T(8,128)}, f32[1,2048]{1,0:T(1,128)}) custom-call(bf16[32,2048]{1,0:T(8,128)(2,1)} %og_h.1, bf16[256,2048]{1,0:T(8,128)(2,1)} %bitcast.7, bf16[2048,256]{1,0:T(8,128)(2,1)} %bitcast.8, bf16[256,2048]{1,0:T(8,128)(2,1)} %bitcast.9, bf16[2048,256]{1,0:T(8,128)(2,1)} %bitcast.10, ...), custom_call_target="tpu_custom_call" | custom-call | tf_op jit(solution)/shard_map/tower_backward/pallas_call | solution.py:286
  72.1 2.5 %place_columns.1 = (bf16[32,16384]{1,0:T(8,128)(2,1)}, f32[8,2048]{1,0:T(8,128)}, f32[1,2048]{1,0:T(1,128)}) custom-call(s32[128]{0:T(128)} %assign_ref.1, bf16[128,32,128]{2,1,0:T(8,128)(2,1)} %bitcast.6, f32[8,2048]{1,0:T(8,128)} %get-tuple-element.10.w_ref, f32[1,2048]{1,0:T(1,128)} %get-tuple-element.11.b_ref), custom_call_target="tpu_custom_call" | custom-call | tf_op jit(solution)/shard_map/place_columns/pallas_call | solution.py:334

commit v2 on v1

v2 whole, which is shorter than its diff:
```python
import functools
import math

import jax
import jax.numpy as jnp
from jax import lax
from jax.experimental import pallas as pl
from jax.experimental.pallas import tpu as pltpu
from jax.sharding import PartitionSpec as P

MESH = pl.DeviceIdType.MESH
F32 = jnp.float32
BF16 = jnp.bfloat16
NX, NYH, NZ, NYL, NC = 4, 2, 12, 4, 2
TOWERS = NX * NYH
EMB = 128
TILE = 512
LONG, SHORT = 6, 5
SUBS = ((0, 0), (0, 1), (1, 0), (1, 1))
NEED = (6, -5, 5, -4, 4, -3, 3, -2, 2, -1, 1, 0)


def dot_nn(a, b):
    return jnp.dot(a, b, preferred_element_type=F32)


def dot_nt(a, b):
    return lax.dot_general(a, b, (((1,), (1,)), ((), ())), preferred_element_type=F32)


def remote(src, dst, send, recv, device):
    return pltpu.make_async_remote_copy(
        src_ref=src, dst_ref=dst, send_sem=send, recv_sem=recv, device_id=device, device_id_type=MESH
    )


def main_kernel(
    scale,
    og_h, x_h, wd_h, wu_h, wo_h, cb_h,
    out_f, out_w, out_b,
    x, wd, wu, wo, cb, go, fac, cr, gc, ggl, gi, part, pair, long_s, long_r, short_s, short_r,
    og, mine, y_s, y_r, bias, b_pair, b_y, b_z, b_half, b_other,
    in_sem, og_sem, a1_s, a1_r, a2_s, a2_r, p_s, p_r, l_s, l_r, s_s, s_r, ys_s, ys_r,
    bp_s, bp_r, by_s, by_r, bz_s, bz_r, bf_s, bf_r,
):
    t = lax.axis_index("tower")
    s = lax.axis_index("shard")
    yh, xx = t // NX, t % NX
    z, yl, c = s // (NYL * NC), (s // NC) % NYL, s % NC
    sign = 1 - 2 * c
    rows, width = x.shape
    tiles = width // TILE
    half = width // 2

    def tower_at(i):
        return ((yh + i // NX) % NYH) * NX + (xx + i % NX) % NX

    def shard_at(zz, yy, cc):
        return {"shard": (zz * NYL + yy) * NC + cc}

    order = [i for i in range(NX, TOWERS)] + [i for i in range(1, NX)]
    partner = shard_at(z, yl, 1 - c)
    peers = [{"tower": tower_at(i)} for i in order]
    peers.append(partner)
    peers += [shard_at(z, (yl + j) % NYL, c) for j in range(1, NYL)]
    peers += [shard_at((z + j) % NZ, yl, c) for j in range(1, NZ)]

    barrier = pltpu.get_barrier_semaphore()
    for peer in peers:
        pl.semaphore_signal(barrier, inc=1, device_id=peer, device_id_type=MESH)

    loads = [
        pltpu.make_async_copy(src, dst, in_sem.at[k])
        for k, (src, dst) in enumerate(((x_h, x), (wd_h, wd), (wu_h, wu), (cb_h, cb), (wo_h, wo)))
    ]
    own = pltpu.make_async_copy(
        og_h.at[:, pl.ds(pl.multiple_of(t * 256, 256), 256)], go.at[t], in_sem.at[5]
    )
    stage = []
    for i in order:
        dest = tower_at(i)
        stage.append(
            pltpu.make_async_copy(og_h.at[:, pl.ds(pl.multiple_of(dest * 256, 256), 256)], og.at[dest], og_sem.at[i])
        )
        stage[-1].start()
    own.start()
    for load in loads:
        load.start()
    for copy in stage:
        copy.wait()
    pl.semaphore_wait(barrier, len(peers))

    first = []
    for i in order:
        dest = tower_at(i)
        first.append(remote(og.at[dest], go.at[t], a1_s.at[i], a1_r.at[i], {"tower": dest}))
        first[-1].start()

    loads[0].wait()
    loads[1].wait()
    hidden_wide = dot_nn(x[...], wd[...]).astype(BF16)
    hidden_t = hidden_wide.astype(F32).T.astype(BF16)
    loads[2].wait()
    loads[3].wait()

    spans = [pl.ds(k * TILE, TILE) for k in range(tiles)]
    for at in spans:
        factor = dot_nn(hidden_wide, wu[:, at]) + cb[:, at] + 1.0
        fac[:, at] = factor
        cr[:, at] = (x[:, at].astype(F32) * factor).astype(BF16)
    loads[4].wait()
    own.wait()
    for copy in first:
        copy.wait_recv()
    grad_out = go[...].reshape(rows, 256)

    def weights(p, left, right):
        for k, at in enumerate(spans):
            q, low = k * TILE // half, k * TILE % half
            value = dot_nn(left, right[:, at])
            for zz in range(4):
                for h in range(2):
                    for cc in range(NC):
                        base = zz * 64 + h * 32 + cc * 8
                        both = jnp.concatenate([value[base : base + 8], value[base + 16 : base + 24]], axis=0)
                        part[cc, p * 4 + zz, h, q, :, low : low + TILE] = both.astype(BF16)

    hidden_grad_wide = jnp.zeros((rows, 256), F32)
    for k, at in enumerate(spans):
        low = dot_nt(grad_out, wo[at, :]).astype(BF16)
        gc[:, at] = low
        gate = low.astype(F32) * x[:, at].astype(F32)
        bias[k * TILE // half, :, k * TILE % half : k * TILE % half + TILE] = jnp.sum(gate, axis=0, keepdims=True)
        gate_low = gate.astype(BF16)
        ggl[:, at] = gate_low
        hidden_grad_wide = hidden_grad_wide + dot_nt(gate_low, wu[:, at])
    hidden_grad = hidden_grad_wide.astype(BF16)
    bias_pair = remote(bias.at[1 - c], b_pair, bp_s, bp_r, partner)
    bias_pair.start()
    weights(2, grad_out.astype(F32).T.astype(BF16), cr)
    weights(1, hidden_t, ggl)
    weights(0, hidden_grad.astype(F32).T.astype(BF16), x)

    def chunk(offset, direction):
        return (z + direction * offset + NZ) % NZ

    pieces = []
    for k, offset in enumerate(NEED):
        pieces.append(
            remote(part.at[1 - c, chunk(offset, -sign)], pair.at[k], p_s.at[k], p_r.at[k], partner)
        )
        pieces[-1].start()

    for k, at in enumerate(spans):
        value = gc[:, at].astype(F32) * fac[:, at] + dot_nt(hidden_grad, wd[at, :])
        low = value.astype(BF16)
        for a in range(TOWERS):
            for j in range(TILE // EMB):
                gi[a, k * (TILE // EMB) + j] = low[a * 32 : (a + 1) * 32, j * EMB : (j + 1) * EMB]
    second = []
    for i in order:
        dest = tower_at(i)
        second.append(remote(gi.at[dest], out_f.at[t], a2_s.at[i], a2_r.at[i], {"tower": dest}))
        second[-1].start()
    keep = pltpu.make_async_copy(gi.at[t], out_f.at[t], in_sem.at[6])
    keep.start()

    ahead = shard_at((z + sign + NZ) % NZ, yl, c)
    behind = shard_at((z - sign + NZ) % NZ, yl, c)

    def local_sum(k, h, q):
        return part[c, chunk(NEED[k], sign), h, q].astype(F32) + pair[k, h, q].astype(F32)

    arms = {
        "long": (long_s, long_r, l_s, l_r, ahead, LONG),
        "short": (short_s, short_r, s_s, s_r, behind, SHORT),
    }
    sent = {}
    bias_y, bias_z = [], []
    for step in range(LONG):
        for name in ("long", "short"):
            if step < arms[name][5]:
                pieces[NEED.index(LONG - step if name == "long" else step - SHORT)].wait_recv()
        for h, q in SUBS:
            for name, (send_ref, recv_ref, send_sem, recv_sem, device, hops) in arms.items():
                if step >= hops:
                    continue
                value = local_sum(NEED.index(hops - step if name == "long" else step - hops), h, q)
                if step > 0:
                    sent[name, step - 1, h, q].wait_recv()
                    value = value + recv_ref[step - 1, h, q].astype(F32)
                send_ref[step, h, q] = value.astype(BF16)
                copy = remote(
                    send_ref.at[step, h, q], recv_ref.at[step, h, q],
                    send_sem.at[step, h * 2 + q], recv_sem.at[step, h * 2 + q], device,
                )
                copy.start()
                sent[name, step, h, q] = copy
        if step == 0:
            bias_pair.wait_recv()
            b_z[z] = bias[c] + b_pair[...]
            for j in range(1, NZ):
                copy = remote(b_z.at[z], b_z.at[z], bz_s.at[j], bz_r.at[j], shard_at((z + j) % NZ, yl, c))
                copy.start()
                bias_z.append(copy)
        if step == 3:
            for copy in bias_z:
                copy.wait_recv()
            column = b_z[0]
            for k in range(1, NZ):
                column = column + b_z[k]
            b_y[yl] = column
            for j in range(1, NYL):
                copy = remote(b_y.at[yl], b_y.at[yl], by_s.at[j], by_r.at[j], shard_at(z, (yl + j) % NYL, c))
                copy.start()
                bias_y.append(copy)

    pieces[len(NEED) - 1].wait_recv()
    for h in range(2):
        halves = []
        for q in range(2):
            value = local_sum(len(NEED) - 1, h, q)
            sent["short", SHORT - 1, h, q].wait_recv()
            value = value + short_r[SHORT - 1, h, q].astype(F32)
            sent["long", LONG - 1, h, q].wait_recv()
            halves.append(value + long_r[LONG - 1, h, q].astype(F32))
        for yy in range(2):
            eight = [value[yy * 8 : (yy + 1) * 8] for value in halves]
            for q in range(2):
                mine[h * 2 + yy, :, q * half : (q + 1) * half] = eight[q]
            y_s[h * 2 + yy] = jnp.concatenate(eight, axis=0).astype(BF16)
    last = []
    for j in range(1, NYL):
        to = (yl + j) % NYL
        copy = remote(y_s.at[to], y_r.at[j - 1], ys_s.at[j], ys_r.at[j], shard_at(z, to, c))
        copy.start()
        last.append(copy)

    for copy in bias_y:
        copy.wait_recv()
    total = (b_y[0] + b_y[1]) + (b_y[2] + b_y[3])
    b_half[...] = total
    bias_final = remote(b_half, b_other, bf_s, bf_r, partner)
    bias_final.start()
    out_b[:, pl.ds(pl.multiple_of(c * half, half), half)] = total

    value = mine[yl]
    for copy in last:
        copy.wait_recv()
    for j in range(NYL - 1):
        got = y_r[j].astype(F32)
        value = value + jnp.concatenate([got[:8], got[8:]], axis=1)
    out_w[...] = value * scale

    bias_final.wait_recv()
    out_b[:, pl.ds(pl.multiple_of((1 - c) * half, half), half)] = b_other[...]

    keep.wait()
    for copy in second:
        copy.wait_recv()
    for copy in first + second + pieces + list(sent.values()) + bias_y + bias_z + last + [bias_pair, bias_final]:
        copy.wait_send()


def place_kernel(assign_ref, f_ref, w_ref, b_ref, out_f, out_w, out_b, slot_of, held, placed, in_sem, out_sem):
    slots = f_ref.shape[0]
    each = slots // TOWERS
    loads = []
    for n in range(TOWERS):
        loads.append(
            pltpu.make_async_copy(f_ref.at[pl.ds(n * each, each)], held.at[pl.ds(n * each, each)], in_sem.at[n])
        )
        loads[-1].start()
    out_w[...] = w_ref[...]
    out_b[...] = b_ref[...]

    def invert(k, carry):
        slot_of[assign_ref[k]] = k
        return carry

    lax.fori_loop(0, slots, invert, 0, unroll=8)
    for load in loads:
        load.wait()
    stores = []
    for n in range(TOWERS):
        for feature in range(n * each, (n + 1) * each):
            placed[:, feature * EMB : (feature + 1) * EMB] = held[slot_of[feature]]
        at = pl.ds(n * each * EMB, each * EMB)
        stores.append(pltpu.make_async_copy(placed.at[:, at], out_f.at[:, at], out_sem.at[n]))
        stores[-1].start()
    for store in stores:
        store.wait()


def body(out_grad, pooled, down_proj, up_proj, cross_bias, out_proj, assign):
    rows, width = pooled.shape[1:]
    any_space = pl.BlockSpec(memory_space=pl.ANY)
    vmem = pl.BlockSpec(memory_space=pltpu.VMEM)
    scale = 1.0 / math.sqrt(rows * lax.axis_size("shard"))
    dma = pltpu.SemaphoreType.DMA
    half = width // 2
    moved, weights, bias = pl.pallas_call(
        functools.partial(main_kernel, scale),
        out_shape=(
            jax.ShapeDtypeStruct((TOWERS, width // EMB, 32, EMB), BF16),
            jax.ShapeDtypeStruct((8, width), F32),
            jax.ShapeDtypeStruct((1, width), F32),
        ),
        in_specs=[any_space] * 6,
        out_specs=(any_space, vmem, vmem),
        scratch_shapes=[
            pltpu.VMEM((rows, width), BF16),
            pltpu.VMEM((width, 256), BF16),
            pltpu.VMEM((256, width), BF16),
            pltpu.VMEM((width, 256), BF16),
            pltpu.VMEM((1, width), F32),
            pltpu.VMEM((TOWERS, 32, 256), BF16),
            pltpu.VMEM((rows, width), F32),
            pltpu.VMEM((rows, width), BF16),
            pltpu.VMEM((rows, width), BF16),
            pltpu.VMEM((rows, width), BF16),
            pltpu.VMEM((TOWERS, width // EMB, 32, EMB), BF16),
            pltpu.VMEM((NC, NZ, 2, 2, 16, half), BF16),
            pltpu.VMEM((NZ, 2, 2, 16, half), BF16),
            pltpu.VMEM((LONG, 2, 2, 16, half), BF16),
            pltpu.VMEM((LONG, 2, 2, 16, half), BF16),
            pltpu.VMEM((SHORT, 2, 2, 16, half), BF16),
            pltpu.VMEM((SHORT, 2, 2, 16, half), BF16),
            pltpu.VMEM((TOWERS, 32, 256), BF16),
            pltpu.VMEM((NYL, 8, width), F32),
            pltpu.VMEM((NYL, 16, half), BF16),
            pltpu.VMEM((NYL - 1, 16, half), BF16),
            pltpu.VMEM((2, 1, half), F32),
            pltpu.VMEM((1, half), F32),
            pltpu.VMEM((NYL, 1, half), F32),
            pltpu.VMEM((NZ, 1, half), F32),
            pltpu.VMEM((1, half), F32),
            pltpu.VMEM((1, half), F32),
            dma((7,)),
            dma((TOWERS,)),
            dma((TOWERS,)), dma((TOWERS,)), dma((TOWERS,)), dma((TOWERS,)),
            dma((NZ,)), dma((NZ,)),
            dma((LONG, 4)), dma((LONG, 4)), dma((SHORT, 4)), dma((SHORT, 4)),
            dma((NYL,)), dma((NYL,)),
            dma, dma, dma((NYL,)), dma((NYL,)), dma((NZ,)), dma((NZ,)), dma, dma,
        ],
        compiler_params=pltpu.CompilerParams(
            collective_id=0, has_side_effects=True, vmem_limit_bytes=65000 * 1024
        ),
        name="tower_backward",
    )(out_grad, pooled[0], down_proj[0], up_proj[0], out_proj[0], cross_bias)
    feature_grad, weight_grad, bias_grad = pl.pallas_call(
        place_kernel,
        out_shape=(
            jax.ShapeDtypeStruct((32, TOWERS * width), BF16),
            jax.ShapeDtypeStruct((8, width), F32),
            jax.ShapeDtypeStruct((1, width), F32),
        ),
        in_specs=[pl.BlockSpec(memory_space=pltpu.SMEM), any_space, vmem, vmem],
        out_specs=(any_space, vmem, vmem),
        scratch_shapes=[
            pltpu.SMEM((TOWERS * (width // EMB),), jnp.int32),
            pltpu.VMEM((TOWERS * (width // EMB), 32, EMB), BF16),
            pltpu.VMEM((32, TOWERS * width), BF16),
            dma((TOWERS,)),
            dma((TOWERS,)),
        ],
        compiler_params=pltpu.CompilerParams(vmem_limit_bytes=65000 * 1024),
        name="place_columns",
    )(assign, moved.reshape(TOWERS * (width // EMB), 32, EMB), weights, bias)
    return (feature_grad, weight_grad[None], bias_grad)


def solution(mesh):
    placed = (
        P(("tower", "shard"), None),
        P("tower", "shard", None),
        P("tower", None, None),
        P("tower", None, None),
        P("tower", None),
        P("tower", None, None),
        P(),
    )
    return jax.shard_map(
        body,
        mesh=mesh,
        in_specs=placed,
        out_specs=(P(("tower", "shard"), None), P("tower", "shard", None), P("tower", None)),
        check_vma=False,
    )
```

time: 75 us -> 61.5 us (0.82)
  Pallas kernels: 73.9 us -> 60.3 us
    pallas_call x1, Pallas kernels: 71.4 us -> 56.4 us  [body(): pl.pallas_call(functools.partial(main_kernel, scale), out_shape=(jax.Shap...]
    pallas_call x1, Pallas kernels: 2.51 us -> 3.88 us  [body(): pl.pallas_call(place_kernel, out_shape=(jax.ShapeDtypeStruct((32, TOWERS...]
where the time goes in v2:
time: 61.5 us; the launch traced here: 60.9 us
  Pallas kernels  60.3 us (98%)
  between operations  0.64 us (1%)
    pallas_call x1, Pallas kernels, body(): pl.pallas_call(functools.partial(main_kernel, scale), out_shape=(jax.Shap...  56.4 us
    pallas_call x1, Pallas kernels, body(): pl.pallas_call(place_kernel, out_shape=(jax.ShapeDtypeStruct((32, TOWERS...  3.88 us

profile of v2, /device:TPU:1, one launch (start us, length us, event | category | flops | bytes accessed | tf_op | source)
XLA Modules:
  0.0 60.9 jit_solution(10851516680255953701)
XLA Ops:
  0.6 56.4 %tower_backward.1 = (bf16[8,16,32,128]{3,2,1,0:T(8,128)(2,1)}, f32[8,2048]{1,0:T(8,128)}, f32[1,2048]{1,0:T(1,128)}) custom-call(bf16[32,2048]{1,0:T(8,128)(2,1)} %og_h.1, bf16[256,2048]{1,0:T(8,128)(2,1)} %bitcast.7, bf16[2048,256]{1,0:T(8,128)(2,1)} %bitcast.8, bf16[256,2048]{1,0:T(8,128)(2,1)} %bitcast.9, bf16[2048,256]{1,0:T(8,128)(2,1)} %bitcast.10, ...), custom_call_target="tpu_custom_call" | custom-call | tf_op jit(solution)/shard_map/tower_backward/pallas_call | solution.py:302
  57.0 3.9 %place_columns.1 = (bf16[32,16384]{1,0:T(8,128)(2,1)}, f32[8,2048]{1,0:T(8,128)}, f32[1,2048]{1,0:T(1,128)}) custom-call(s32[128]{0:T(128)} %assign_ref.1, bf16[128,32,128]{2,1,0:T(8,128)(2,1)} %bitcast.6, f32[8,2048]{1,0:T(8,128)} %get-tuple-element.10.w_ref, f32[1,2048]{1,0:T(1,128)} %get-tuple-element.11.b_ref), custom_call_target="tpu_custom_call" | custom-call | tf_op jit(solution)/shard_map/place_columns/pallas_call | solution.py:352

commit v3 on v2

--- a/solution.py
+++ b/solution.py
@@ -58,7 +58,7 @@
     def shard_at(zz, yy, cc):
         return {"shard": (zz * NYL + yy) * NC + cc}
 
-    order = [i for i in range(NX, TOWERS)] + [i for i in range(1, NX)]
+    order = (6, 5, 7, 4, 2, 1, 3)
     partner = shard_at(z, yl, 1 - c)
     peers = [{"tower": tower_at(i)} for i in order]
     peers.append(partner)
@@ -262,34 +262,11 @@
         copy.wait_send()
 
 
-def place_kernel(assign_ref, f_ref, w_ref, b_ref, out_f, out_w, out_b, slot_of, held, placed, in_sem, out_sem):
-    slots = f_ref.shape[0]
-    each = slots // TOWERS
-    loads = []
-    for n in range(TOWERS):
-        loads.append(
-            pltpu.make_async_copy(f_ref.at[pl.ds(n * each, each)], held.at[pl.ds(n * each, each)], in_sem.at[n])
-        )
-        loads[-1].start()
+def place_kernel(assign_ref, f_ref, w_ref, b_ref, out_f, out_w, out_b):
+    for k in range(f_ref.shape[0]):
+        out_f[:, pl.ds(pl.multiple_of(assign_ref[k] * EMB, EMB), EMB)] = f_ref[k]
     out_w[...] = w_ref[...]
     out_b[...] = b_ref[...]
-
-    def invert(k, carry):
-        slot_of[assign_ref[k]] = k
-        return carry
-
-    lax.fori_loop(0, slots, invert, 0, unroll=8)
-    for load in loads:
-        load.wait()
-    stores = []
-    for n in range(TOWERS):
-        for feature in range(n * each, (n + 1) * each):
-            placed[:, feature * EMB : (feature + 1) * EMB] = held[slot_of[feature]]
-        at = pl.ds(n * each * EMB, each * EMB)
-        stores.append(pltpu.make_async_copy(placed.at[:, at], out_f.at[:, at], out_sem.at[n]))
-        stores[-1].start()
-    for store in stores:
-        store.wait()
 
 
 def body(out_grad, pooled, down_proj, up_proj, cross_bias, out_proj, assign):
@@ -356,16 +333,8 @@
             jax.ShapeDtypeStruct((8, width), F32),
             jax.ShapeDtypeStruct((1, width), F32),
         ),
-        in_specs=[pl.BlockSpec(memory_space=pltpu.SMEM), any_space, vmem, vmem],
-        out_specs=(any_space, vmem, vmem),
-        scratch_shapes=[
-            pltpu.SMEM((TOWERS * (width // EMB),), jnp.int32),
-            pltpu.VMEM((TOWERS * (width // EMB), 32, EMB), BF16),
-            pltpu.VMEM((32, TOWERS * width), BF16),
-            dma((TOWERS,)),
-            dma((TOWERS,)),
-        ],
-        compiler_params=pltpu.CompilerParams(vmem_limit_bytes=65000 * 1024),
+        in_specs=[pl.BlockSpec(memory_space=pltpu.SMEM), vmem, vmem, vmem],
+        out_specs=(vmem, vmem, vmem),
         name="place_columns",
     )(assign, moved.reshape(TOWERS * (width // EMB), 32, EMB), weights, bias)
     return (feature_grad, weight_grad[None], bias_grad)

time: 61.5 us -> 60 us (0.976)
  Pallas kernels: 60.3 us -> 58.5 us
    pallas_call x1, Pallas kernels: 3.88 us -> 2.51 us  [body(): pl.pallas_call(place_kernel, out_shape=(jax.ShapeDtypeStruct((32, TOWERS...]
where the time goes in v3:
time: 60 us; the launch traced here: 59.2 us
  Pallas kernels  58.5 us (98%)
  between operations  0.64 us (1%)
    pallas_call x1, Pallas kernels, body(): pl.pallas_call(functools.partial(main_kernel, scale), out_shape=(jax.Shap...  56 us
    pallas_call x1, Pallas kernels, body(): pl.pallas_call(place_kernel, out_shape=(jax.ShapeDtypeStruct((32, TOWERS...  2.51 us

profile of v3, /device:TPU:1, one launch (start us, length us, event | category | flops | bytes accessed | tf_op | source)
XLA Modules:
  0.0 59.2 jit_solution(1792054671311321492)
XLA Ops:
  0.6 56.0 %tower_backward.1 = (bf16[8,16,32,128]{3,2,1,0:T(8,128)(2,1)}, f32[8,2048]{1,0:T(8,128)}, f32[1,2048]{1,0:T(1,128)}) custom-call(bf16[32,2048]{1,0:T(8,128)(2,1)} %og_h.1, bf16[256,2048]{1,0:T(8,128)(2,1)} %bitcast.7, bf16[2048,256]{1,0:T(8,128)(2,1)} %bitcast.8, bf16[256,2048]{1,0:T(8,128)(2,1)} %bitcast.9, bf16[2048,256]{1,0:T(8,128)(2,1)} %bitcast.10, ...), custom_call_target="tpu_custom_call" | custom-call | tf_op jit(solution)/shard_map/tower_backward/pallas_call | solution.py:279
  56.7 2.5 %place_columns.1 = (bf16[32,16384]{1,0:T(8,128)(2,1)}, f32[8,2048]{1,0:T(8,128)}, f32[1,2048]{1,0:T(1,128)}) custom-call(s32[128]{0:T(128)} %assign_ref.1, bf16[128,32,128]{2,1,0:T(8,128)(2,1)} %bitcast.6, f32[8,2048]{1,0:T(8,128)} %get-tuple-element.10.w_ref, f32[1,2048]{1,0:T(1,128)} %get-tuple-element.11.b_ref), custom_call_target="tpu_custom_call" | custom-call | tf_op jit(solution)/shard_map/place_columns/pallas_call | solution.py:329

commit v4 on v3

--- a/solution.py
+++ b/solution.py
@@ -16,7 +16,6 @@
 EMB = 128
 TILE = 512
 LONG, SHORT = 6, 5
-SUBS = ((0, 0), (0, 1), (1, 0), (1, 1))
 NEED = (6, -5, 5, -4, 4, -3, 3, -2, 2, -1, 1, 0)
 
 
@@ -39,8 +38,8 @@
     og_h, x_h, wd_h, wu_h, wo_h, cb_h,
     out_f, out_w, out_b,
     x, wd, wu, wo, cb, go, fac, cr, gc, ggl, gi, part, pair, long_s, long_r, short_s, short_r,
-    og, mine, y_s, y_r, bias, b_pair, b_y, b_z, b_half, b_other,
-    in_sem, og_sem, a1_s, a1_r, a2_s, a2_r, p_s, p_r, l_s, l_r, s_s, s_r, ys_s, ys_r,
+    og, f_s, f_r, mine, y_s, y_r, bias, b_pair, b_y, b_z, b_half, b_other,
+    in_sem, og_sem, a1_s, a1_r, a2_s, a2_r, p_s, p_r, l_s, l_r, s_s, s_r, ys_s, ys_r, fs_s, fs_r,
     bp_s, bp_r, by_s, by_r, bz_s, bz_r, bf_s, bf_r,
 ):
     t = lax.axis_index("tower")
@@ -64,6 +63,7 @@
     peers.append(partner)
     peers += [shard_at(z, (yl + j) % NYL, c) for j in range(1, NYL)]
     peers += [shard_at((z + j) % NZ, yl, c) for j in range(1, NZ)]
+    peers += [shard_at((z + d) % NZ, (yl + j) % NYL, c) for d in (1, NZ - 1) for j in range(1, NYL)]
 
     barrier = pltpu.get_barrier_semaphore()
     for peer in peers:
@@ -165,8 +165,7 @@
     keep = pltpu.make_async_copy(gi.at[t], out_f.at[t], in_sem.at[6])
     keep.start()
 
-    ahead = shard_at((z + sign + NZ) % NZ, yl, c)
-    behind = shard_at((z - sign + NZ) % NZ, yl, c)
+    ahead, behind = (z + sign + NZ) % NZ, (z - sign + NZ) % NZ
 
     def local_sum(k, h, q):
         return part[c, chunk(NEED[k], sign), h, q].astype(F32) + pair[k, h, q].astype(F32)
@@ -176,26 +175,61 @@
         "short": (short_s, short_r, s_s, s_r, behind, SHORT),
     }
     sent = {}
-    bias_y, bias_z = [], []
+    bias_y, bias_z, last = [], [], []
+
+    def eights(values, yy):
+        return jnp.concatenate([value[yy * 8 : (yy + 1) * 8] for value in values], axis=0).astype(BF16)
+
+    def whole(got):
+        wide = got.astype(F32)
+        return jnp.concatenate([wide[:8], wide[8:]], axis=1)
+
     for step in range(LONG):
         for name in ("long", "short"):
             if step < arms[name][5]:
                 pieces[NEED.index(LONG - step if name == "long" else step - SHORT)].wait_recv()
-        for h, q in SUBS:
-            for name, (send_ref, recv_ref, send_sem, recv_sem, device, hops) in arms.items():
+        for h in range(2):
+            for arm, (name, (send_ref, recv_ref, send_sem, recv_sem, to, hops)) in enumerate(arms.items()):
                 if step >= hops:
                     continue
-                value = local_sum(NEED.index(hops - step if name == "long" else step - hops), h, q)
-                if step > 0:
-                    sent[name, step - 1, h, q].wait_recv()
-                    value = value + recv_ref[step - 1, h, q].astype(F32)
-                send_ref[step, h, q] = value.astype(BF16)
-                copy = remote(
-                    send_ref.at[step, h, q], recv_ref.at[step, h, q],
-                    send_sem.at[step, h * 2 + q], recv_sem.at[step, h * 2 + q], device,
-                )
+                values = []
+                for q in range(2):
+                    value = local_sum(NEED.index(hops - step if name == "long" else step - hops), h, q)
+                    if step > 0:
+                        sent[name, step - 1, h, q].wait_recv()
+                        value = value + recv_ref[step - 1, h, q].astype(F32)
+                    values.append(value)
+                    if step < hops - 1:
+                        send_ref[step, h, q] = value.astype(BF16)
+                        copy = remote(
+                            send_ref.at[step, h, q], recv_ref.at[step, h, q],
+                            send_sem.at[step, h * 2 + q], recv_sem.at[step, h * 2 + q], shard_at(to, yl, c),
+                        )
+                        copy.start()
+                        sent[name, step, h, q] = copy
+                if step == hops - 1:
+                    for yy in range(2):
+                        row = h * 2 + yy
+                        f_s[arm, row] = eights(values, yy)
+                        copy = remote(
+                            f_s.at[arm, row], f_r.at[arm, yl],
+                            fs_s.at[arm, row], fs_r.at[arm, yl], shard_at(to, row, c),
+                        )
+                        copy.start()
+                        sent[name, step, row] = copy
+        if step == 1:
+            pieces[len(NEED) - 1].wait_recv()
+            for h in range(2):
+                values = [local_sum(len(NEED) - 1, h, q) for q in range(2)]
+                for yy in range(2):
+                    y_s[h * 2 + yy] = eights(values, yy)
+                    for q in range(2):
+                        mine[h * 2 + yy, :, q * half : (q + 1) * half] = values[q][yy * 8 : (yy + 1) * 8]
+            for j in range(1, NYL):
+                to = (yl + j) % NYL
+                copy = remote(y_s.at[to], y_r.at[j - 1], ys_s.at[j], ys_r.at[j], shard_at(z, to, c))
                 copy.start()
-                sent[name, step, h, q] = copy
+                last.append(copy)
         if step == 0:
             bias_pair.wait_recv()
             b_z[z] = bias[c] + b_pair[...]
@@ -215,27 +249,14 @@
                 copy.start()
                 bias_y.append(copy)
 
-    pieces[len(NEED) - 1].wait_recv()
-    for h in range(2):
-        halves = []
-        for q in range(2):
-            value = local_sum(len(NEED) - 1, h, q)
-            sent["short", SHORT - 1, h, q].wait_recv()
-            value = value + short_r[SHORT - 1, h, q].astype(F32)
-            sent["long", LONG - 1, h, q].wait_recv()
-            halves.append(value + long_r[LONG - 1, h, q].astype(F32))
-        for yy in range(2):
-            eight = [value[yy * 8 : (yy + 1) * 8] for value in halves]
-            for q in range(2):
-                mine[h * 2 + yy, :, q * half : (q + 1) * half] = eight[q]
-            y_s[h * 2 + yy] = jnp.concatenate(eight, axis=0).astype(BF16)
-    last = []
-    for j in range(1, NYL):
-        to = (yl + j) % NYL
-        copy = remote(y_s.at[to], y_r.at[j - 1], ys_s.at[j], ys_r.at[j], shard_at(z, to, c))
-        copy.start()
-        last.append(copy)
-
+    value = mine[yl]
+    for copy in last:
+        copy.wait_recv()
+    for j in range(NYL - 1):
+        value = value + whole(y_r[j])
+    for k in range(NYL):
+        remote(f_s.at[1, k], f_r.at[1, k], fs_s.at[1, k], fs_r.at[1, k], partner).wait_recv()
+        value = value + whole(f_r[1, k])
     for copy in bias_y:
         copy.wait_recv()
     total = (b_y[0] + b_y[1]) + (b_y[2] + b_y[3])
@@ -244,12 +265,9 @@
     bias_final.start()
     out_b[:, pl.ds(pl.multiple_of(c * half, half), half)] = total
 
-    value = mine[yl]
-    for copy in last:
-        copy.wait_recv()
-    for j in range(NYL - 1):
-        got = y_r[j].astype(F32)
-        value = value + jnp.concatenate([got[:8], got[8:]], axis=1)
+    for k in range(NYL):
+        remote(f_s.at[0, k], f_r.at[0, k], fs_s.at[0, k], fs_r.at[0, k], partner).wait_recv()
+        value = value + whole(f_r[0, k])
     out_w[...] = value * scale
 
     bias_final.wait_recv()
@@ -304,6 +322,8 @@
             pltpu.VMEM((SHORT, 2, 2, 16, half), BF16),
             pltpu.VMEM((SHORT, 2, 2, 16, half), BF16),
             pltpu.VMEM((TOWERS, 32, 256), BF16),
+            pltpu.VMEM((2, NYL, 16, half), BF16),
+            pltpu.VMEM((2, NYL, 16, half), BF16),
             pltpu.VMEM((NYL, 8, width), F32),
             pltpu.VMEM((NYL, 16, half), BF16),
             pltpu.VMEM((NYL - 1, 16, half), BF16),
@@ -318,7 +338,7 @@
             dma((TOWERS,)), dma((TOWERS,)), dma((TOWERS,)), dma((TOWERS,)),
             dma((NZ,)), dma((NZ,)),
             dma((LONG, 4)), dma((LONG, 4)), dma((SHORT, 4)), dma((SHORT, 4)),
-            dma((NYL,)), dma((NYL,)),
+            dma((NYL,)), dma((NYL,)), dma((2, NYL)), dma((2, NYL)),
             dma, dma, dma((NYL,)), dma((NYL,)), dma((NZ,)), dma((NZ,)), dma, dma,
         ],
         compiler_params=pltpu.CompilerParams(

time: 60 us -> 68.3 us (1.14); the launches traced: 59.2 us -> 68.2 us
  Pallas kernels: 58.5 us -> 67.5 us
    pallas_call x1, Pallas kernels: 56 us -> 65 us  [body(): pl.pallas_call(functools.partial(main_kernel, scale), out_shape=(jax.Shap...]
where the time goes in v4:
time: 68.3 us; the launch traced here: 68.2 us
  Pallas kernels  67.5 us (99%)
    pallas_call x1, Pallas kernels, body(): pl.pallas_call(functools.partial(main_kernel, scale), out_shape=(jax.Shap...  65 us
    pallas_call x1, Pallas kernels, body(): pl.pallas_call(place_kernel, out_shape=(jax.ShapeDtypeStruct((32, TOWERS...  2.51 us

profile of v4, /device:TPU:1, one launch (start us, length us, event | category | flops | bytes accessed | tf_op | source)
XLA Modules:
  0.0 68.2 jit_solution(15888610383819290459)
XLA Ops:
  0.6 65.0 %tower_backward.1 = (bf16[8,16,32,128]{3,2,1,0:T(8,128)(2,1)}, f32[8,2048]{1,0:T(8,128)}, f32[1,2048]{1,0:T(1,128)}) custom-call(bf16[32,2048]{1,0:T(8,128)(2,1)} %og_h.1, bf16[256,2048]{1,0:T(8,128)(2,1)} %bitcast.7, bf16[2048,256]{1,0:T(8,128)(2,1)} %bitcast.8, bf16[256,2048]{1,0:T(8,128)(2,1)} %bitcast.9, bf16[2048,256]{1,0:T(8,128)(2,1)} %bitcast.10, ...), custom_call_target="tpu_custom_call" | custom-call | tf_op jit(solution)/shard_map/tower_backward/pallas_call | solution.py:297
  65.7 2.5 %place_columns.1 = (bf16[32,16384]{1,0:T(8,128)(2,1)}, f32[8,2048]{1,0:T(8,128)}, f32[1,2048]{1,0:T(1,128)}) custom-call(s32[128]{0:T(128)} %assign_ref.1, bf16[128,32,128]{2,1,0:T(8,128)(2,1)} %bitcast.6, f32[8,2048]{1,0:T(8,128)} %get-tuple-element.10.w_ref, f32[1,2048]{1,0:T(1,128)} %get-tuple-element.11.b_ref), custom_call_target="tpu_custom_call" | custom-call | tf_op jit(solution)/shard_map/place_columns/pallas_call | solution.py:349

commit v5 on v3

--- a/solution.py
+++ b/solution.py
@@ -177,7 +177,8 @@
     }
     sent = {}
     bias_y, bias_z = [], []
-    for step in range(LONG):
+    ahead2 = shard_at((z + 2 * sign + NZ) % NZ, yl, c)
+    for step in range(SHORT):
         for name in ("long", "short"):
             if step < arms[name][5]:
                 pieces[NEED.index(LONG - step if name == "long" else step - SHORT)].wait_recv()
@@ -190,12 +191,24 @@
                     sent[name, step - 1, h, q].wait_recv()
                     value = value + recv_ref[step - 1, h, q].astype(F32)
                 send_ref[step, h, q] = value.astype(BF16)
+                to = ahead2 if name == "long" and step == SHORT - 1 else device
                 copy = remote(
                     send_ref.at[step, h, q], recv_ref.at[step, h, q],
-                    send_sem.at[step, h * 2 + q], recv_sem.at[step, h * 2 + q], device,
+                    send_sem.at[step, h * 2 + q], recv_sem.at[step, h * 2 + q], to,
                 )
                 copy.start()
                 sent[name, step, h, q] = copy
+        if step == 1:
+            near = NEED.index(1)
+            pieces[near].wait_recv()
+            for h, q in SUBS:
+                long_s[LONG - 1, h, q] = local_sum(near, h, q).astype(BF16)
+                copy = remote(
+                    long_s.at[LONG - 1, h, q], long_r.at[LONG - 1, h, q],
+                    l_s.at[LONG - 1, h * 2 + q], l_r.at[LONG - 1, h * 2 + q], ahead,
+                )
+                copy.start()
+                sent["near", 0, h, q] = copy
         if step == 0:
             bias_pair.wait_recv()
             b_z[z] = bias[c] + b_pair[...]
@@ -222,8 +235,10 @@
             value = local_sum(len(NEED) - 1, h, q)
             sent["short", SHORT - 1, h, q].wait_recv()
             value = value + short_r[SHORT - 1, h, q].astype(F32)
-            sent["long", LONG - 1, h, q].wait_recv()
-            halves.append(value + long_r[LONG - 1, h, q].astype(F32))
+            sent["near", 0, h, q].wait_recv()
+            value = value + long_r[LONG - 1, h, q].astype(F32)
+            sent["long", SHORT - 1, h, q].wait_recv()
+            halves.append(value + long_r[SHORT - 1, h, q].astype(F32))
         for yy in range(2):
             eight = [value[yy * 8 : (yy + 1) * 8] for value in halves]
             for q in range(2):

time: 60 us -> 61.6 us (1.027); the launches traced: 59.2 us -> 61.5 us
  Pallas kernels: 58.5 us -> 60.8 us
    pallas_call x1, Pallas kernels: 56 us -> 58.3 us  [body(): pl.pallas_call(functools.partial(main_kernel, scale), out_shape=(jax.Shap...]
where the time goes in v5:
time: 61.6 us; the launch traced here: 61.5 us
  Pallas kernels  60.8 us (99%)
  between operations  0.64 us (1%)
    pallas_call x1, Pallas kernels, body(): pl.pallas_call(functools.partial(main_kernel, scale), out_shape=(jax.Shap...  58.3 us
    pallas_call x1, Pallas kernels, body(): pl.pallas_call(place_kernel, out_shape=(jax.ShapeDtypeStruct((32, TOWERS...  2.51 us

profile of v5, /device:TPU:1, one launch (start us, length us, event | category | flops | bytes accessed | tf_op | source)
XLA Modules:
  0.0 61.5 jit_solution(2173168293781079911)
XLA Ops:
  0.6 58.3 %tower_backward.1 = (bf16[8,16,32,128]{3,2,1,0:T(8,128)(2,1)}, f32[8,2048]{1,0:T(8,128)}, f32[1,2048]{1,0:T(1,128)}) custom-call(bf16[32,2048]{1,0:T(8,128)(2,1)} %og_h.1, bf16[256,2048]{1,0:T(8,128)(2,1)} %bitcast.7, bf16[2048,256]{1,0:T(8,128)(2,1)} %bitcast.8, bf16[256,2048]{1,0:T(8,128)(2,1)} %bitcast.9, bf16[2048,256]{1,0:T(8,128)(2,1)} %bitcast.10, ...), custom_call_target="tpu_custom_call" | custom-call | tf_op jit(solution)/shard_map/tower_backward/pallas_call | solution.py:294
  59.0 2.5 %place_columns.1 = (bf16[32,16384]{1,0:T(8,128)(2,1)}, f32[8,2048]{1,0:T(8,128)}, f32[1,2048]{1,0:T(1,128)}) custom-call(s32[128]{0:T(128)} %assign_ref.1, bf16[128,32,128]{2,1,0:T(8,128)(2,1)} %bitcast.6, f32[8,2048]{1,0:T(8,128)} %get-tuple-element.10.w_ref, f32[1,2048]{1,0:T(1,128)} %get-tuple-element.11.b_ref), custom_call_target="tpu_custom_call" | custom-call | tf_op jit(solution)/shard_map/place_columns/pallas_call | solution.py:344

commit v6 on v3

--- a/solution.py
+++ b/solution.py
@@ -151,6 +151,14 @@
         )
         pieces[-1].start()
 
+    bias_z = []
+    bias_pair.wait_recv()
+    b_z[z] = bias[c] + b_pair[...]
+    for j in range(1, NZ):
+        copy = remote(b_z.at[z], b_z.at[z], bz_s.at[j], bz_r.at[j], shard_at((z + j) % NZ, yl, c))
+        copy.start()
+        bias_z.append(copy)
+
     for k, at in enumerate(spans):
         value = gc[:, at].astype(F32) * fac[:, at] + dot_nt(hidden_grad, wd[at, :])
         low = value.astype(BF16)
@@ -176,7 +184,7 @@
         "short": (short_s, short_r, s_s, s_r, behind, SHORT),
     }
     sent = {}
-    bias_y, bias_z = [], []
+    bias_y = []
     for step in range(LONG):
         for name in ("long", "short"):
             if step < arms[name][5]:
@@ -196,13 +204,6 @@
                 )
                 copy.start()
                 sent[name, step, h, q] = copy
-        if step == 0:
-            bias_pair.wait_recv()
-            b_z[z] = bias[c] + b_pair[...]
-            for j in range(1, NZ):
-                copy = remote(b_z.at[z], b_z.at[z], bz_s.at[j], bz_r.at[j], shard_at((z + j) % NZ, yl, c))
-                copy.start()
-                bias_z.append(copy)
         if step == 3:
             for copy in bias_z:
                 copy.wait_recv()

time: 60 us -> 61 us (1.017); the launches traced: 59.2 us -> 60.8 us
  Pallas kernels: 58.5 us -> 60.2 us
    pallas_call x1, Pallas kernels: 56 us -> 57.6 us  [body(): pl.pallas_call(functools.partial(main_kernel, scale), out_shape=(jax.Shap...]
where the time goes in v6:
time: 61 us; the launch traced here: 60.8 us
  Pallas kernels  60.2 us (99%)
  between operations  0.64 us (1%)
    pallas_call x1, Pallas kernels, body(): pl.pallas_call(functools.partial(main_kernel, scale), out_shape=(jax.Shap...  57.6 us
    pallas_call x1, Pallas kernels, body(): pl.pallas_call(place_kernel, out_shape=(jax.ShapeDtypeStruct((32, TOWERS...  2.51 us

profile of v6, /device:TPU:1, one launch (start us, length us, event | category | flops | bytes accessed | tf_op | source)
XLA Modules:
  0.0 60.8 jit_solution(17284289825362000503)
XLA Ops:
  0.6 57.6 %tower_backward.1 = (bf16[8,16,32,128]{3,2,1,0:T(8,128)(2,1)}, f32[8,2048]{1,0:T(8,128)}, f32[1,2048]{1,0:T(1,128)}) custom-call(bf16[32,2048]{1,0:T(8,128)(2,1)} %og_h.1, bf16[256,2048]{1,0:T(8,128)(2,1)} %bitcast.7, bf16[2048,256]{1,0:T(8,128)(2,1)} %bitcast.8, bf16[256,2048]{1,0:T(8,128)(2,1)} %bitcast.9, bf16[2048,256]{1,0:T(8,128)(2,1)} %bitcast.10, ...), custom_call_target="tpu_custom_call" | custom-call | tf_op jit(solution)/shard_map/tower_backward/pallas_call | solution.py:280
  58.3 2.5 %place_columns.1 = (bf16[32,16384]{1,0:T(8,128)(2,1)}, f32[8,2048]{1,0:T(8,128)}, f32[1,2048]{1,0:T(1,128)}) custom-call(s32[128]{0:T(128)} %assign_ref.1, bf16[128,32,128]{2,1,0:T(8,128)(2,1)} %bitcast.6, f32[8,2048]{1,0:T(8,128)} %get-tuple-element.10.w_ref, f32[1,2048]{1,0:T(1,128)} %get-tuple-element.11.b_ref), custom_call_target="tpu_custom_call" | custom-call | tf_op jit(solution)/shard_map/place_columns/pallas_call | solution.py:330

commit v7 on v6

--- a/solution.py
+++ b/solution.py
@@ -151,13 +151,13 @@
         )
         pieces[-1].start()
 
-    bias_z = []
+    bias_y = []
     bias_pair.wait_recv()
-    b_z[z] = bias[c] + b_pair[...]
-    for j in range(1, NZ):
-        copy = remote(b_z.at[z], b_z.at[z], bz_s.at[j], bz_r.at[j], shard_at((z + j) % NZ, yl, c))
+    b_y[yl] = bias[c] + b_pair[...]
+    for j in range(1, NYL):
+        copy = remote(b_y.at[yl], b_y.at[yl], by_s.at[j], by_r.at[j], shard_at(z, (yl + j) % NYL, c))
         copy.start()
-        bias_z.append(copy)
+        bias_y.append(copy)
 
     for k, at in enumerate(spans):
         value = gc[:, at].astype(F32) * fac[:, at] + dot_nt(hidden_grad, wd[at, :])
@@ -184,7 +184,7 @@
         "short": (short_s, short_r, s_s, s_r, behind, SHORT),
     }
     sent = {}
-    bias_y = []
+    bias_z = []
     for step in range(LONG):
         for name in ("long", "short"):
             if step < arms[name][5]:
@@ -205,17 +205,14 @@
                 copy.start()
                 sent[name, step, h, q] = copy
         if step == 3:
-            for copy in bias_z:
+            for copy in bias_y:
                 copy.wait_recv()
-            column = b_z[0]
-            for k in range(1, NZ):
-                column = column + b_z[k]
-            b_y[yl] = column
-            for j in range(1, NYL):
-                copy = remote(b_y.at[yl], b_y.at[yl], by_s.at[j], by_r.at[j], shard_at(z, (yl + j) % NYL, c))
-                copy.start()
-                bias_y.append(copy)
-
+            b_z[z] = (b_y[0] + b_y[1]) + (b_y[2] + b_y[3])
+
+    for j in range(1, NZ):
+        copy = remote(b_z.at[z], b_z.at[z], bz_s.at[j], bz_r.at[j], shard_at((z + j) % NZ, yl, c))
+        copy.start()
+        bias_z.append(copy)
     pieces[len(NEED) - 1].wait_recv()
     for h in range(2):
         halves = []
@@ -237,9 +234,11 @@
         copy.start()
         last.append(copy)
 
-    for copy in bias_y:
+    for copy in bias_z:
         copy.wait_recv()
-    total = (b_y[0] + b_y[1]) + (b_y[2] + b_y[3])
+    total = b_z[0]
+    for k in range(1, NZ):
+        total = total + b_z[k]
     b_half[...] = total
     bias_final = remote(b_half, b_other, bf_s, bf_r, partner)
     bias_final.start()

time: 61 us -> 62.5 us (1.025); the launches traced: 60.8 us -> 61.4 us
  no operation moved by 1% of the time
where the time goes in v7:
time: 62.5 us; the launch traced here: 61.4 us
  Pallas kernels  60.7 us (97%)
  between operations  0.64 us (1%)
    pallas_call x1, Pallas kernels, body(): pl.pallas_call(functools.partial(main_kernel, scale), out_shape=(jax.Shap...  58.2 us
    pallas_call x1, Pallas kernels, body(): pl.pallas_call(place_kernel, out_shape=(jax.ShapeDtypeStruct((32, TOWERS...  2.51 us

profile of v7, /device:TPU:1, one launch (start us, length us, event | category | flops | bytes accessed | tf_op | source)
XLA Modules:
  0.0 61.4 jit_solution(8461839970110174139)
XLA Ops:
  0.6 58.2 %tower_backward.1 = (bf16[8,16,32,128]{3,2,1,0:T(8,128)(2,1)}, f32[8,2048]{1,0:T(8,128)}, f32[1,2048]{1,0:T(1,128)}) custom-call(bf16[32,2048]{1,0:T(8,128)(2,1)} %og_h.1, bf16[256,2048]{1,0:T(8,128)(2,1)} %bitcast.7, bf16[2048,256]{1,0:T(8,128)(2,1)} %bitcast.8, bf16[256,2048]{1,0:T(8,128)(2,1)} %bitcast.9, bf16[2048,256]{1,0:T(8,128)(2,1)} %bitcast.10, ...), custom_call_target="tpu_custom_call" | custom-call | tf_op jit(solution)/shard_map/tower_backward/pallas_call | solution.py:279
  58.8 2.5 %place_columns.1 = (bf16[32,16384]{1,0:T(8,128)(2,1)}, f32[8,2048]{1,0:T(8,128)}, f32[1,2048]{1,0:T(1,128)}) custom-call(s32[128]{0:T(128)} %assign_ref.1, bf16[128,32,128]{2,1,0:T(8,128)(2,1)} %bitcast.6, f32[8,2048]{1,0:T(8,128)} %get-tuple-element.10.w_ref, f32[1,2048]{1,0:T(1,128)} %get-tuple-element.11.b_ref), custom_call_target="tpu_custom_call" | custom-call | tf_op jit(solution)/shard_map/place_columns/pallas_call | solution.py:329
